TPU v7x, 128 devices: a whole 4x4x4 slice. The times are simulated.
128 devices in a mesh: modes: 16 (over z_lo, y, core), tiles: 8 (over z_hi, x).
Axes of the slice: x: 4, y: 4, z: 4 (z_hi: 2, z_lo: 2; z = z_hi * 2 + z_lo), core: 2. Of those that a mesh axis runs over, the one named last changes fastest.
Arguments:
- solution_modes: float32 [512, 32, 8, 128], P('modes', 'tiles'), may hold values from -6 to 6
- coefficient_modes: float32 [128, 32, 8, 128], P('modes', 'tiles'), may hold values from 0.5 to 4
- coupling: float32 [16, 32, 32, 32], P('modes'), may hold values from -0.03125 to 0.03125
- source_block: int32 [16, 32], P('modes'), may hold values from 0 to 15
- expansion_index: int32 [16, 32], P('modes'), may hold values from 0 to 127
Outputs:
- applied: float32 [512, 32, 8, 128], P('modes', 'tiles')
All inputs are finite; a program needn't handle non-finite values.
Results may differ from a plain program's by a relative error of at most 0.0003.
Values sent between devices are 32-bit elements; how exact they have to be, the bound alone decides.
A program may use at most 128 MiB of HBM per device.

v0:
```python
import jax
import jax.numpy as jnp
from jax import lax
from jax.sharding import PartitionSpec as P


def with_halo(value, sides, width):
    for axis, dim in sides:
        count, length = (lax.axis_size(axis), value.shape[dim])
        up = [(i, (i + 1) % count) for i in range(count - 1)]
        down = [(j, i) for i, j in up]
        last = lax.slice_in_dim(value, length - width, length, axis=dim)
        initial = lax.slice_in_dim(value, 0, width, axis=dim)
        before = lax.ppermute(last, axis, up)
        after = lax.ppermute(initial, axis, down)
        value = jnp.concatenate([before, value, after], axis=dim)
    return value


def face_means(coefficient):
    along_first = 0.5 * (coefficient[:, :-1, 1:-1, 1:-1] + coefficient[:, 1:, 1:-1, 1:-1])
    along_second = 0.5 * (coefficient[:, 1:-1, :-1, 1:-1] + coefficient[:, 1:-1, 1:, 1:-1])
    along_third = 0.5 * (coefficient[:, 1:-1, 1:-1, :-1] + coefficient[:, 1:-1, 1:-1, 1:])
    return (along_first, along_second, along_third)


def divergence(blended, along_first, along_second, along_third):
    flux_first = along_first * (blended[:, :-1, 1:-1, 1:-1] - blended[:, 1:, 1:-1, 1:-1])
    flux_second = along_second * (blended[:, 1:-1, :-1, 1:-1] - blended[:, 1:-1, 1:, 1:-1])
    flux_third = along_third * (blended[:, 1:-1, 1:-1, :-1] - blended[:, 1:-1, 1:-1, 1:])
    result = flux_first[:, 1:] - flux_first[:, :-1]
    result = result + flux_second[:, :, 1:] - flux_second[:, :, :-1]
    return result + flux_third[:, :, :, 1:] - flux_third[:, :, :, :-1]


def slot_term(padded_u, faces, block_matrix, offset, expansion, width):
    first_faces, second_faces, third_faces = faces
    source_modes = lax.dynamic_slice_in_dim(padded_u, offset * width, width, 0)
    blended = jnp.einsum(
        "ij,jxyz->ixyz", block_matrix, source_modes, precision=lax.Precision.HIGHEST
    )
    return divergence(
        blended,
        lax.dynamic_index_in_dim(first_faces, expansion, 0, keepdims=False),
        lax.dynamic_index_in_dim(second_faces, expansion, 0, keepdims=False),
        lax.dynamic_index_in_dim(third_faces, expansion, 0, keepdims=False),
    )


def block_output(padded_u, faces, coupling_rows, source_rows, expansion_rows, width):
    shape = (width, padded_u.shape[1] - 2, padded_u.shape[2] - 2, padded_u.shape[3] - 2)

    def advance(running, slot_index):
        source = source_rows[slot_index]
        expansion = expansion_rows[slot_index]
        term = slot_term(padded_u, faces, coupling_rows[slot_index], source, expansion, width)
        return (running + term, None)

    start = jnp.zeros(shape, jnp.float32)
    total, _ = lax.scan(advance, start, jnp.arange(source_rows.shape[0], dtype=jnp.int32))
    return total


def on_device(solution_modes, coefficient_modes, coupling, source_block, expansion_index):
    local_solution = solution_modes.shape[0]
    local_coefficient = coefficient_modes.shape[0]
    width = coupling.shape[2]
    groups = lax.axis_size("modes")
    padding = ((0, 0), (0, 0), (1, 1), (1, 1))
    stacked = jnp.concatenate([solution_modes, coefficient_modes], axis=0)
    rimmed = with_halo(stacked, (("tiles", 1),), 1)
    everyone = lax.all_gather(rimmed, "modes", axis=0, tiled=True)
    trailing = everyone.shape[1:]
    shaped = everyone.reshape((groups, local_solution + local_coefficient) + trailing)
    all_solution = shaped[:, :local_solution].reshape((groups * local_solution,) + trailing)
    all_coefficient = shaped[:, local_solution:].reshape((groups * local_coefficient,) + trailing)
    padded_u = jnp.pad(all_solution, padding)
    padded_a = jnp.pad(all_coefficient, padding)
    faces = face_means(padded_a)
    outputs = block_output(padded_u, faces, coupling[0], source_block[0], expansion_index[0], width)
    return outputs


def solution(mesh):
    placed = (
        P("modes", "tiles", None, None),
        P("modes", "tiles", None, None),
        P("modes", None, None, None),
        P("modes", None),
        P("modes", None),
    )
    return jax.shard_map(
        on_device,
        mesh=mesh,
        in_specs=placed,
        out_specs=P("modes", "tiles", None, None),
        check_vma=False,
    )
```

profile of v0, /device:TPU:1, one launch (start us, length us, event | category | flops | bytes accessed | tf_op | source)
XLA Modules:
  0.0 699.4 jit_solution(3090703868489263197)
XLA Ops:
  9.9 4.6 collective-permute-start
  17.7 95.7 %all-gather.2.cloned.1.call-done = f32[640,6,8,128]{3,2,1,0:T(8,128)} async-done(((f32[40,6,8,128]{3,2,1,0:T(8,128)}), f32[640,6,8,128]{3,2,1,0:T(8,128)}) %all-gather.2.cloned.1.call-update) | async-done | bytes 15728656 | tf_op jit(solution)/shard_map/all_gather | solution.py:72
  115.6 10.5 %slice.107 = f32[16,32,6,8,128]{4,3,2,1,0:T(8,128)} slice(f32[16,40,6,8,128]{4,3,2,1,0:T(8,128)} %bitcast.41), slice={[0:16], [0:32], [0:6], [0:8], [0:128]} | slice | bytes 25165824 | tf_op jit(solution)/shard_map/slice | solution.py:75
  127.9 2.7 fusion.10
  130.6 3.1 fusion.12
  133.7 13.2 %copy.8 = f32[16,32,6,8,128]{4,1,0,3,2:T(8,128)} copy(f32[16,32,6,8,128]{4,3,2,1,0:T(8,128)} %slice.107) | data formatting | bytes 25165824 | tf_op jit(solution)/shard_map/slice | solution.py:75
  146.9 15.0 %pad.8 = f32[512,6,10,130]{3,0,2,1:T(8,128)} pad(f32[512,6,8,128]{3,0,2,1:T(8,128)} %bitcast.39, f32[]{:T(128)} %constant.32.clone.1), padding=0_0x0_0x1_1x1_1 | pad | bytes 28557316 | tf_op jit(solution)/shard_map/jit(_pad)/pad | solution.py:77
  162.0 528.5 %while.11 = (s32[]{:T(128)}, f32[32,4,8,128]{3,0,2,1:T(8,128)}, s32[32]{0:T(128)S(1)}, s32[32]{0:T(128)S(1)}, f32[128,5,8,128]{3,2,1,0:T(8,128)}, /*index=5*/f32...) while((s32[]{:T(128)}, f32[32,4,8,128]{3,0,2,1:T(8,128)}, ...), condition=%wide.region_1.2_spmd.clone, body=%wide.region_0.1_spmd.clone.sunk | while | flops 97650696 | bytes 12662481 | solution.py:60
  165.7 3.3 fusion.24
  182.1 3.3 fusion.24
  192.3 2.6 fusion.28
  198.6 3.3 fusion.24
  208.8 2.6 fusion.28
  215.1 3.3 fusion.24
  225.3 2.6 fusion.28
  231.6 3.3 fusion.24
  241.8 2.6 fusion.28
  248.2 3.3 fusion.24
  258.3 2.6 fusion.28
  264.7 3.3 fusion.24
  274.9 2.6 fusion.28
  281.2 3.3 fusion.24
  291.4 2.6 fusion.28
  297.7 3.3 fusion.24
  307.9 2.6 fusion.28
  314.2 3.3 fusion.24
  324.4 2.6 fusion.28
  330.7 3.3 fusion.24
  347.3 3.3 fusion.24
  363.8 3.3 fusion.24
  374.0 2.6 fusion.28
  380.3 3.3 fusion.24
  390.5 2.6 fusion.28
  396.8 3.3 fusion.24
  407.0 2.6 fusion.28
  413.3 3.3 fusion.24
  423.5 2.6 fusion.28
  429.9 3.3 fusion.24
  440.0 2.6 fusion.28
  446.4 3.3 fusion.24
  456.6 2.6 fusion.28
  462.9 3.3 fusion.24
  473.1 2.6 fusion.28
  479.4 3.3 fusion.24
  495.9 3.3 fusion.24
  506.1 2.6 fusion.28
  512.4 3.3 fusion.24
  522.6 2.6 fusion.28
  529.0 3.3 fusion.24
  545.5 3.3 fusion.24
  555.7 2.6 fusion.28
  562.0 3.3 fusion.24
  578.5 3.3 fusion.24
  588.7 2.6 fusion.28
  595.0 3.3 fusion.24
  605.2 2.6 fusion.28
  611.6 3.3 fusion.24
  621.7 2.6 fusion.28
  628.1 3.3 fusion.24
  638.3 2.6 fusion.28
  644.6 3.3 fusion.24
  654.8 2.6 fusion.28
  661.1 3.3 fusion.24
  677.6 3.3 fusion.24
  (314 shorter events, 233.5 us)
Async XLA Ops:
  6.5 106.9 %all-gather.2.cloned.1.call-start = ((), (), s32[]{:S(2)}) async-start(), calls=%async_computation | async-start | bytes 16711680 | tf_op jit(solution)/shard_map/all_gather | solution.py:72
  8.6 7.4 %collective-permute-start.1 = (f32[40,1,8,128]{3,2,1,0:T(8,128)S(1)}, f32[40,1,8,128]{3,2,1,0:T(8,128)S(1)}, u32[]{:S(2)}, u32[]{:S(2)}) collective-permute-start(f32[40,1,8,128]{3,2,1,0:T(8,128)S(1)} %get-tuple-element.112), channel_id=1, source_target_pairs={{1,0},{2,1},{3,2},{4,3},{5,4},{6,5},{7,6},{9,8},{10,9},{11,10},{12... | collective-permute-start | bytes 491528 | tf_op jit(solution)/shard_map/ppermute | solution.py:15
  9.9 6.8 collective-permute-start
  146.9 15.0 %copy-start = (s32[1,32]{1,0:T(1,128)S(1)}, s32[1,32]{1,0:T(1,128)}, u32[]{:S(2)}) copy-start(s32[1,32]{1,0:T(1,128)} %param.11) | copy-start | bytes 388
  146.9 15.0 %copy-start.1 = (s32[1,32]{1,0:T(1,128)S(1)}, s32[1,32]{1,0:T(1,128)}, u32[]{:S(2)}) copy-start(s32[1,32]{1,0:T(1,128)} %param.10) | copy-start | bytes 388
Sparse Core Ops, SparseCore 0:
  17.8 95.5 all-gather.1
where the time goes:
time: 710 us; the launch traced here: 699 us
  local copies, waits for them, and re-layouts  177 us (25%)
  other arithmetic  161 us (23%)
  loops' own time  138 us (19%)
  matrix products  106 us (15%)
  waiting for transfers between devices  97.9 us (14%)
  between operations  13.4 us (2%)
    another operation x1, loops' own time, block_output(): lax.scan(advance, start, jnp.arange(source_rows.shape[0], dtype=jnp.int32))  138 us
    dot_general x32, matrix products, slot_term(): jnp.einsum('ij,jxyz->ixyz', block_matrix, source_modes, precision=lax.Pre...  106 us
    all_gather x1, waiting for transfers between devices, on_device(): everyone = lax.all_gather(rimmed, 'modes', axis=0, tiled=True)  95.7 us
    add x32, other arithmetic, advance(): return (running + term, None)  84.6 us
    mul x32, other arithmetic, divergence(): along_third * (blended[:, 1:-1, 1:-1, :-1] - blended[:, 1:-1, 1:-1, 1:])  42.9 us
    mul x32, local copies, waits for them, and re-layouts, divergence(): along_third * (blended[:, 1:-1, 1:-1, :-1] - blended[:, 1:-1, 1:-1, 1:])  24.5 us
    mul x32, local copies, waits for them, and re-layouts, divergence(): along_second * (blended[:, 1:-1, :-1, 1:-1] - blended[:, 1:-1, 1:, 1:-1])  24.3 us
    slice x2, local copies, waits for them, and re-layouts, on_device(): shaped[:, :local_solution].reshape((groups * local_solution,) + trailing)  23.7 us
  transfers between devices with their start and end apart: 3, of which 3 were waited for; matrix products, arithmetic and copies ran while one was open for 0% of the time, Pallas kernels for 0%

commit v1 on v0

--- a/solution.py
+++ b/solution.py
@@ -2,6 +2,11 @@
 import jax.numpy as jnp
 from jax import lax
 from jax.sharding import PartitionSpec as P
+
+
+def exchange_gather(array, mesh_axis, dim):
+    sent = jnp.stack([array] * lax.axis_size(mesh_axis))
+    return jnp.concatenate(lax.all_to_all(sent, mesh_axis, 0, 0), axis=dim)
 
 
 def with_halo(value, sides, width):
@@ -69,7 +74,7 @@
     padding = ((0, 0), (0, 0), (1, 1), (1, 1))
     stacked = jnp.concatenate([solution_modes, coefficient_modes], axis=0)
     rimmed = with_halo(stacked, (("tiles", 1),), 1)
-    everyone = lax.all_gather(rimmed, "modes", axis=0, tiled=True)
+    everyone = exchange_gather(rimmed, "modes", 0)
     trailing = everyone.shape[1:]
     shaped = everyone.reshape((groups, local_solution + local_coefficient) + trailing)
     all_solution = shaped[:, :local_solution].reshape((groups * local_solution,) + trailing)

time: 710 us -> 850 us (1.20)
  the two profiles are of different devices: /device:TPU:1 before, /device:TPU:73 now
where the time goes in v1:
time: 850 us; the launch traced here: 839 us
  waiting for transfers between devices  220 us (26%)
  local copies, waits for them, and re-layouts  187 us (22%)
  other arithmetic  160 us (19%)
  loops' own time  152 us (18%)
  matrix products  106 us (12%)
  starting transfers between devices  13.7 us (2%)
    all_to_all x1, waiting for transfers between devices, exchange_gather(): return jnp.concatenate(lax.all_to_all(sent, mesh_axis, 0, 0), axis=dim)  211 us
    another operation x1, loops' own time, block_output(): lax.scan(advance, start, jnp.arange(source_rows.shape[0], dtype=jnp.int32))  152 us
    dot_general x32, matrix products, slot_term(): jnp.einsum('ij,jxyz->ixyz', block_matrix, source_modes, precision=lax.Pre...  106 us
    add x32, other arithmetic, advance(): return (running + term, None)  84.7 us
    mul x32, other arithmetic, divergence(): along_third * (blended[:, 1:-1, 1:-1, :-1] - blended[:, 1:-1, 1:-1, 1:])  43 us
    mul x32, local copies, waits for them, and re-layouts, divergence(): along_third * (blended[:, 1:-1, 1:-1, :-1] - blended[:, 1:-1, 1:-1, 1:])  24.5 us
    mul x32, local copies, waits for them, and re-layouts, divergence(): along_second * (blended[:, 1:-1, :-1, 1:-1] - blended[:, 1:-1, 1:, 1:-1])  24.3 us
    slice x2, local copies, waits for them, and re-layouts, on_device(): shaped[:, :local_solution].reshape((groups * local_solution,) + trailing)  23.7 us
  transfers between devices with their start and end apart: 3, of which 3 were waited for; matrix products, arithmetic and copies ran while one was open for 0% of the time, Pallas kernels for 0%

profile of v1, /device:TPU:73, one launch (start us, length us, event | category | flops | bytes accessed | tf_op | source)
XLA Modules:
  0.0 839.1 jit_solution(17193200246665808145)
XLA Ops:
  2.0 3.5 collective-permute-start.1
  9.0 6.8 collective-permute-done
  15.9 7.0 stack.2
  22.9 8.3 all-to-all-start
  31.2 211.2 %all-to-all-done = f32[16,40,6,8,128]{4,3,2,1,0:T(8,128)} async-done(((f32[16,40,6,8,128]{4,3,2,1,0:T(8,128)}), f32[16,40,6,8,128]{4,3,2,1,0:T(8,128)}, u32[]{:S(2)}, u32[]{:S(2)}) %all-to-all-start) | async-done | bytes 15728672 | tf_op jit(solution)/shard_map/all_to_all | solution.py:9
  246.5 2.7 fusion.10
  249.2 3.1 fusion.12
  252.3 10.5 %slice.107 = f32[16,32,6,8,128]{4,3,2,1,0:T(8,128)} slice(f32[16,40,6,8,128]{4,3,2,1,0:T(8,128)} %all-to-all-done), slice={[0:16], [0:32], [0:6], [0:8], [0:128]} | slice | bytes 25165824 | tf_op jit(solution)/shard_map/slice | solution.py:80
  262.8 13.2 %copy.6 = f32[16,32,6,8,128]{4,1,0,3,2:T(8,128)} copy(f32[16,32,6,8,128]{4,3,2,1,0:T(8,128)} %slice.107) | data formatting | bytes 25165824 | tf_op jit(solution)/shard_map/slice | solution.py:80
  276.0 15.0 %pad.8 = f32[512,6,10,130]{3,0,2,1:T(8,128)} pad(f32[512,6,8,128]{3,0,2,1:T(8,128)} %bitcast.38, f32[]{:T(128)} %constant.32.clone.1), padding=0_0x0_0x1_1x1_1 | pad | bytes 28557316 | tf_op jit(solution)/shard_map/jit(_pad)/pad | solution.py:82
  291.0 545.9 %while.11 = (s32[]{:T(128)}, f32[32,4,8,128]{3,0,2,1:T(8,128)}, s32[32]{0:T(128)S(1)}, s32[32]{0:T(128)S(1)}, f32[128,5,8,128]{3,2,1,0:T(8,128)}, /*index=5*/f32...) while((s32[]{:T(128)}, f32[32,4,8,128]{3,0,2,1:T(8,128)}, ...), condition=%wide.region_1.2_spmd.clone, body=%wide.region_0.1_spmd.clone.sunk | while | flops 97650696 | bytes 12662481 | solution.py:65
  295.0 3.3 fusion.24
  312.0 3.3 fusion.24
  322.4 2.7 fusion.28
  329.0 3.3 fusion.24
  339.4 2.7 fusion.28
  346.1 3.3 fusion.24
  356.5 2.7 fusion.28
  363.2 3.3 fusion.24
  373.6 2.7 fusion.28
  380.2 3.3 fusion.24
  390.6 2.7 fusion.28
  397.3 3.3 fusion.24
  414.3 3.3 fusion.24
  424.8 2.7 fusion.28
  431.4 3.3 fusion.24
  441.8 2.7 fusion.28
  448.5 3.3 fusion.24
  458.9 2.7 fusion.28
  465.5 3.3 fusion.24
  475.9 2.7 fusion.28
  482.6 3.3 fusion.24
  493.0 2.7 fusion.28
  499.7 3.3 fusion.24
  516.7 3.3 fusion.24
  527.1 2.7 fusion.28
  533.8 3.3 fusion.24
  544.2 2.7 fusion.28
  550.9 3.3 fusion.24
  567.9 3.3 fusion.24
  578.3 2.7 fusion.28
  585.0 3.3 fusion.24
  602.0 3.3 fusion.24
  619.1 3.3 fusion.24
  629.5 2.7 fusion.28
  636.2 3.3 fusion.24
  646.6 2.7 fusion.28
  653.2 3.3 fusion.24
  663.6 2.7 fusion.28
  670.3 3.3 fusion.24
  680.7 2.7 fusion.28
  687.4 3.3 fusion.24
  704.4 3.3 fusion.24
  721.5 3.3 fusion.24
  738.5 3.3 fusion.24
  755.6 3.3 fusion.24
  766.0 2.7 fusion.28
  772.7 3.3 fusion.24
  783.1 2.7 fusion.28
  789.7 3.3 fusion.24
  800.1 2.7 fusion.28
  806.8 3.3 fusion.24
  817.2 2.7 fusion.28
  823.9 3.3 fusion.24
  (314 shorter events, 243.6 us)
Async XLA Ops:
  2.0 7.0 collective-permute-start.1
  5.5 10.3 %collective-permute-start = (f32[40,1,8,128]{3,2,1,0:T(8,128)S(1)}, f32[40,1,8,128]{3,2,1,0:T(8,128)S(1)}, u32[]{:S(2)}, u32[]{:S(2)}) collective-permute-start(f32[40,1,8,128]{3,2,1,0:T(8,128)S(1)} %get-tuple-element.111), channel_id=1, source_target_pairs={{0,1},{1,2},{2,3},{3,4},{4,5},{5,6},{6,7},{8,9},{9,10},{10,11},{11... | collective-permute-start | bytes 491528 | tf_op jit(solution)/shard_map/ppermute | solution.py:19
  22.9 219.5 %all-to-all-start = ((f32[16,40,6,8,128]{4,3,2,1,0:T(8,128)}), f32[16,40,6,8,128]{4,3,2,1,0:T(8,128)}, u32[]{:S(2)}, u32[]{:S(2)}) async-start(f32[16,40,6,8,128]{4,3,2,1,0:T(8,128)} %stack.2), calls=%async_computation | async-start | bytes 31457280 | tf_op jit(solution)/shard_map/all_to_all | solution.py:9
  276.0 15.0 %copy-start = (s32[1,32]{1,0:T(1,128)S(1)}, s32[1,32]{1,0:T(1,128)}, u32[]{:S(2)}) copy-start(s32[1,32]{1,0:T(1,128)} %param.11) | copy-start | bytes 388
  276.0 15.0 %copy-start.1 = (s32[1,32]{1,0:T(1,128)S(1)}, s32[1,32]{1,0:T(1,128)}, u32[]{:S(2)}) copy-start(s32[1,32]{1,0:T(1,128)} %param.10) | copy-start | bytes 388
